TPU v7x, 768 devices: a whole 4x8x12 slice. The times are simulated.
768 devices in a mesh: seq: 16 (over y, core), cp: 48 (over z, x).
Axes of the slice: x: 4, y: 8, z: 12, core: 2. Of those that a mesh axis runs over, the one named last changes fastest.
Arguments:
- query: bfloat16 [98304, 4608], P(('seq', 'cp')), may hold values from -6 to 6
- key_proj: bfloat16 [98304, 4608], P(('seq', 'cp')), may hold values from -6 to 6
- value_proj: bfloat16 [98304, 4608], P(('seq', 'cp')), may hold values from -6 to 6
- featurizer: float32 [3, 7, 288], replicated, may hold values from -2 to 2
- rates: float32 [16, 4608], replicated, may hold values from 2.5431316e-06 to 0.25
- residues: float32 [16, 4608], replicated, may hold values from -5 to 5
- skip: float32 [4608], replicated, may hold values from -4 to 4
Outputs:
- operator_out: bfloat16 [98304, 4608], P(('seq', 'cp'))
All inputs are finite; a program needn't handle non-finite values.
Results may differ from a plain program's by a relative error of at most 0.0064.
Values may be sent and summed in bfloat16 or wider, within the bound.
A program may use at most 128 MiB of HBM per device.

v0:
```python
import math

import jax
import jax.numpy as jnp
from jax import lax
from jax.sharding import PartitionSpec as P

precise = lax.Precision.HIGHEST


def from_behind(value, axis, steps):
    count = lax.axis_size(axis)
    first, last = (max(0, -steps), min(count, count - steps))
    return lax.ppermute(value, axis, [(source, source + steps) for source in range(first, last)])


def prefix(value, axis, join, neutral):
    count, mine = (lax.axis_size(axis), lax.axis_index(axis))
    pieces = jax.tree.map(lambda part: lax.all_gather(part, axis), value)
    so_far = jax.tree.map(
        lambda part, zero: jnp.full_like(part, 0) + jnp.asarray(zero, part.dtype), value, neutral
    )

    def lap(position, so_far):
        longer = join(so_far, jax.tree.map(lambda part: part[position], pieces))
        return jax.tree.map(lambda new, old: jnp.where(position < mine, new, old), longer, so_far)

    return lax.fori_loop(0, count - 1, lap, so_far)


def mode_terms(decay_rate, residue_part):
    mode_count = decay_rate.shape[1]
    return residue_part * jnp.sqrt(-jnp.expm1(-2.0 * decay_rate) / mode_count)


def short_conv(extended, tap_table, row_count):
    tap_count = tap_table.shape[0]
    running = jnp.zeros((row_count, extended.shape[1]), jnp.float32)
    for lag_index in range(tap_count):
        first_row = tap_count - 1 - lag_index
        running = running + tap_table[lag_index][None, :] * extended[
            first_row : first_row + row_count
        ].astype(jnp.float32)
    return running


def link_blocks(earlier, later):
    return (earlier[0] * later[0], later[0] * earlier[1] + later[1])


def modal_local(signal, decay_rate, mode_coef, block_len):
    row_count, chan_count = signal.shape
    block_count = row_count // block_len
    blocks = signal.reshape(block_count, block_len, chan_count)
    offsets = jnp.arange(block_len, dtype=jnp.float32)
    falloff = jnp.exp(-decay_rate[None, :, :] * offsets[:, None, None])
    kernel = jnp.sum(mode_coef[None] * falloff, axis=2)
    lag_table = (
        jnp.arange(block_len, dtype=jnp.int32)[:, None]
        - jnp.arange(block_len, dtype=jnp.int32)[None, :]
    )
    toeplitz = jnp.where((lag_table >= 0)[:, :, None], kernel[jnp.maximum(lag_table, 0)], 0.0)
    within = jnp.einsum("ijc,bjc->bic", toeplitz, blocks, precision=precise)
    block_state = jnp.einsum("jcr,bjc->bcr", falloff[::-1], blocks, precision=precise)
    factor = jnp.broadcast_to(jnp.exp(-decay_rate * block_len)[None], block_state.shape)
    _, through = lax.associative_scan(link_blocks, (factor, block_state))
    entering = jnp.concatenate([jnp.zeros_like(through[:1]), through[:-1]], axis=0)
    leading = mode_coef[None] * falloff * jnp.exp(-decay_rate)[None]
    carried = jnp.einsum("icr,bcr->bic", leading, entering, precision=precise)
    return ((within + carried).reshape(row_count, chan_count), through[-1])


def modal_all(signal, decay_rate, mode_coef):
    row_count, chan_count = signal.shape
    chan_block = math.gcd(chan_count, 128)
    block_total = chan_count // chan_block
    block_len = min(row_count, 32)
    pieces = signal.reshape(row_count, block_total, chan_block).transpose(1, 0, 2)

    def modal_one_block(packed):
        return modal_local(packed[0], packed[1], packed[2], block_len)

    within, end_state = lax.map(
        modal_one_block,
        (
            pieces,
            decay_rate.reshape(block_total, chan_block, -1),
            mode_coef.reshape(block_total, chan_block, -1),
        ),
    )
    return (
        within.transpose(1, 0, 2).reshape(row_count, chan_count),
        end_state.reshape(chan_count, -1),
    )


def incoming(enter_state, decay_rate, mode_coef, row_count):
    chan_count = enter_state.shape[0]
    chan_block = math.gcd(chan_count, 128)
    block_total = chan_count // chan_block
    block_len = min(row_count, 128)

    def incoming_one_block(packed):
        state_part, rate_part, coef_part = packed
        offsets = jnp.arange(block_len, dtype=jnp.float32)
        leading = coef_part[None] * jnp.exp(-rate_part[None] * (offsets[:, None, None] + 1.0))
        starts = jnp.arange(row_count // block_len, dtype=jnp.float32) * block_len
        entering = jnp.exp(-rate_part[None] * starts[:, None, None]) * state_part[None]
        return jnp.einsum("icr,bcr->bic", leading, entering, precision=precise).reshape(
            row_count, chan_block
        )

    pieces = lax.map(
        incoming_one_block,
        (
            enter_state.reshape(block_total, chan_block, -1),
            decay_rate.reshape(block_total, chan_block, -1),
            mode_coef.reshape(block_total, chan_block, -1),
        ),
    )
    return pieces.transpose(1, 0, 2).reshape(row_count, chan_count)


def local(query, key_proj, value_proj, featurizer, rates, residues, skip):
    row_count, feature_width = query.shape
    tap_count = featurizer.shape[1]
    filters = jnp.repeat(featurizer, feature_width // featurizer.shape[2], axis=2)
    tail_start = row_count - tap_count + 1
    received = from_behind(
        (query[tail_start:], key_proj[tail_start:], value_proj[tail_start:]), ("seq", "cp"), 1
    )
    featured = []
    for member, source in enumerate((query, key_proj, value_proj)):
        extended = jnp.concatenate([received[member], source], axis=0)
        featured.append(short_conv(extended, filters[member], row_count))
    gate_half = featured[0].astype(jnp.bfloat16)
    gate = lax.optimization_barrier(gate_half).astype(jnp.float32)
    signal_half = (featured[1] * featured[2]).astype(jnp.bfloat16)
    rate_all = rates.T
    coef_all = mode_terms(rate_all, residues.T)
    unit = jnp.ones((), jnp.float32)
    nothing = jnp.zeros((), jnp.float32)
    owned = feature_width // lax.axis_size("cp")
    col_start = lax.axis_index("cp") * owned
    decay_rate = lax.dynamic_slice_in_dim(rate_all, col_start, owned, 0)
    mode_coef = lax.dynamic_slice_in_dim(coef_all, col_start, owned, 0)
    skip_part = lax.dynamic_slice_in_dim(skip, col_start, owned, 0)
    grouped = lax.all_to_all(signal_half, "cp", split_axis=1, concat_axis=0, tiled=True)
    group_rows = grouped.shape[0]
    signal = grouped.astype(jnp.float32)
    within, end_state = modal_all(signal, decay_rate, mode_coef)

    def link_groups(earlier, later):
        return (
            earlier[0] + later[0],
            jnp.exp(-decay_rate * (group_rows * later[0][..., None, None])) * earlier[1] + later[1],
        )

    prior = prefix((unit, end_state), "seq", link_groups, (nothing, jnp.zeros_like(end_state)))
    convolved = (
        within + incoming(prior[1], decay_rate, mode_coef, group_rows) + skip_part[None, :] * signal
    )
    conv_half = lax.all_to_all(
        convolved.astype(jnp.bfloat16), "cp", split_axis=0, concat_axis=1, tiled=True
    )
    return (gate * conv_half.astype(jnp.float32)).astype(jnp.bfloat16)


def solution(mesh):
    placed = (
        P(("seq", "cp"), None),
        P(("seq", "cp"), None),
        P(("seq", "cp"), None),
        P(),
        P(),
        P(),
        P(),
    )
    return jax.shard_map(
        local, mesh=mesh, in_specs=placed, out_specs=P(("seq", "cp"), None), check_vma=False
    )
```

profile of v0, /device:TPU:56, one launch (start us, length us, event | category | flops | bytes accessed | tf_op | source)
XLA Modules:
  0.0 600.7 jit_solution(3742860335855890919)
XLA Ops:
  1.6 3.4 collective-permute-start.2
  6.6 3.4 collective-permute-start.1
  33.8 2.4 copy.255
  36.1 23.7 %multiply_convert_fusion = bf16[128,4608]{0,1:T(8,128)(2,1)} fusion(bf16[128,4608]{0,1:T(8,128)(2,1)S(1)} %copy.254, bf16[128,4608]{0,1:T(8,128)(2,1)S(1)} %copy.251, bf16[6,4608]{0,1:T(8,128)(2,1)} %copy.255, bf16[6,4608]{0,1:T(8,128)(2,1)S(1)} %copy.252, f32[4608]{0:T(1024)} %broadcast_in_dim.176, f32[4608]{0:T(1024)} %broadcast_in_dim.174, ...), kind=kLoop, calls=%fused_computation.124 | loop fusion | flops 46006272 | bytes 3907584 | tf_op jit(solution)/shard_map/convert_element_type | solution.py:138
  59.9 17.9 %all-to-all-start = ((bf16[128,48,96]{0,2,1:T(8,128)(2,1)}), bf16[128,48,96]{0,2,1:T(8,128)(2,1)S(1)}, u32[]{:S(2)}, u32[]{:S(2)}) async-start(bf16[128,48,96]{0,2,1:T(8,128)(2,1)} %bitcast.11), calls=%async_computation | async-start | bytes 2359296 | tf_op jit(solution)/shard_map/all_to_all | solution.py:148
  84.9 22.4 %all-reduce.15 = f32[16]{0:T(128)} all-reduce(f32[16]{0:T(128)S(1)} %dynamic-update-slice), channel_id=1, replica_groups=mesh['seq'=16,'cp'=48] {'seq'}, use_global_device_ids=true, to_apply=%add.15 | all-reduce | flops 16 | bytes 128
  107.2 15.7 %all-to-all-done = bf16[128,48,96]{0,2,1:T(8,128)(2,1)S(1)} async-done(((bf16[128,48,96]{0,2,1:T(8,128)(2,1)}), bf16[128,48,96]{0,2,1:T(8,128)(2,1)S(1)}, u32[]{:S(2)}, u32[]{:S(2)}) %all-to-all-start) | async-done | bytes 1179680 | tf_op jit(solution)/shard_map/all_to_all | solution.py:148
  127.8 323.7 %while.38 = (s32[]{:T(128)}, f32[3,6144,32]{1,2,0:T(8,128)}, f32[3,32,16]{1,0,2:T(4,128)}, f32[3,6144,32]{1,2,0:T(8,128)}, f32[3,32,16]{2,1,0:T(8,128)}, /*index...) while((s32[]{:T(128)}, f32[3,6144,32]{1,2,0:T(8,128)}, f32[3,32,16]{1,0,2:T(4,128)}, ...), condition=%wide.region_2.3_spmd, body=%wide.region_0.2_spmd.sunk | while | flops 152104448 | bytes 27627892 | solution.py:83
  130.3 2.8 gather_fusion
  136.4 2.1 reshape.267
  138.5 5.8 fusion.89
  144.4 6.8 %fusion.88 = f32[32,192,32]{1,2,0:T(8,128)} fusion(f32[192,32,32]{1,0,2:T(8,128)S(1)} %reshape.267, f32[32,32,32]{1,0,2:T(8,128)S(1)} %copy-done.1, pred[32,32]{1,0:T(8,128)(4,1)S(1)} %subtract_compare_fusion.2), kind=kOutput, calls=%fused_computation.29.clone.1 | convolution fusion | flops 75530240 | bytes 1704960 | tf_op jit(solution)/shard_map/while/body/eval_jaxpr/ijc,bjc->bic/dot_general | solution.py:63
  160.0 29.7 %pad.288 = f32[191,32,16]{1,2,0:T(8,128)} pad(f32[96,32,16]{1,2,0:T(8,128)S(1)} %add.402, f32[]{:T(128)} %constant.89.clone.1..sunk), padding=0_0_1x0_0_0x0_0_0 | pad | bytes 587780 | tf_op jit(solution)/shard_map/while
  191.8 29.7 %pad.286 = f32[192,32,16]{1,2,0:T(8,128)} pad(f32[96,32,16]{1,2,0:T(8,128)S(1)} %add.402, f32[]{:T(128)} %constant.89.clone.1..sunk), padding=1_0_1x0_0_0x0_0_0 | pad | bytes 589828 | tf_op jit(solution)/shard_map/while/body/eval_jaxpr/pad | solution.py:66
  221.5 2.8 slice_add_fusion.25
  224.3 2.3 copy.287
  226.7 2.6 fusion.96
  231.3 2.3 broadcast_in_dim.192
  233.6 2.1 constant_dynamic-update-slice_fusion.4
  238.2 2.8 gather_fusion
  244.3 2.1 reshape.267
  246.5 5.8 fusion.89
  252.3 6.8 %fusion.88 = f32[32,192,32]{1,2,0:T(8,128)} fusion(f32[192,32,32]{1,0,2:T(8,128)S(1)} %reshape.267, f32[32,32,32]{1,0,2:T(8,128)S(1)} %copy-done.1, pred[32,32]{1,0:T(8,128)(4,1)S(1)} %subtract_compare_fusion.2), kind=kOutput, calls=%fused_computation.29.clone.1 | convolution fusion | flops 75530240 | bytes 1704960 | tf_op jit(solution)/shard_map/while/body/eval_jaxpr/ijc,bjc->bic/dot_general | solution.py:63
  267.9 29.7 %pad.288 = f32[191,32,16]{1,2,0:T(8,128)} pad(f32[96,32,16]{1,2,0:T(8,128)S(1)} %add.402, f32[]{:T(128)} %constant.89.clone.1..sunk), padding=0_0_1x0_0_0x0_0_0 | pad | bytes 587780 | tf_op jit(solution)/shard_map/while
  299.7 29.7 %pad.286 = f32[192,32,16]{1,2,0:T(8,128)} pad(f32[96,32,16]{1,2,0:T(8,128)S(1)} %add.402, f32[]{:T(128)} %constant.89.clone.1..sunk), padding=1_0_1x0_0_0x0_0_0 | pad | bytes 589828 | tf_op jit(solution)/shard_map/while/body/eval_jaxpr/pad | solution.py:66
  329.4 2.8 slice_add_fusion.25
  332.2 2.3 copy.287
  334.6 2.6 fusion.96
  339.2 2.3 broadcast_in_dim.192
  346.1 2.8 gather_fusion
  352.2 2.1 reshape.267
  354.3 5.8 fusion.89
  360.1 6.8 %fusion.88 = f32[32,192,32]{1,2,0:T(8,128)} fusion(f32[192,32,32]{1,0,2:T(8,128)S(1)} %reshape.267, f32[32,32,32]{1,0,2:T(8,128)S(1)} %copy-done.1, pred[32,32]{1,0:T(8,128)(4,1)S(1)} %subtract_compare_fusion.2), kind=kOutput, calls=%fused_computation.29.clone.1 | convolution fusion | flops 75530240 | bytes 1704960 | tf_op jit(solution)/shard_map/while/body/eval_jaxpr/ijc,bjc->bic/dot_general | solution.py:63
  375.8 29.7 %pad.288 = f32[191,32,16]{1,2,0:T(8,128)} pad(f32[96,32,16]{1,2,0:T(8,128)S(1)} %add.402, f32[]{:T(128)} %constant.89.clone.1..sunk), padding=0_0_1x0_0_0x0_0_0 | pad | bytes 587780 | tf_op jit(solution)/shard_map/while
  407.6 29.7 %pad.286 = f32[192,32,16]{1,2,0:T(8,128)} pad(f32[96,32,16]{1,2,0:T(8,128)S(1)} %add.402, f32[]{:T(128)} %constant.89.clone.1..sunk), padding=1_0_1x0_0_0x0_0_0 | pad | bytes 589828 | tf_op jit(solution)/shard_map/while/body/eval_jaxpr/pad | solution.py:66
  437.3 2.8 slice_add_fusion.25
  440.1 2.3 copy.287
  442.4 2.6 fusion.96
  447.1 2.3 broadcast_in_dim.192
  452.3 15.3 %all_gather.7 = f32[16,96,16]{1,2,0:T(8,128)S(1)} all-gather(f32[1,96,16]{1,2,0:T(8,128)S(1)} %all_gather_reshape.3), channel_id=1, replica_groups=mesh['seq'=16,'cp'=48] {'seq'}, dimensions={0}, use_global_device_ids=true | all-gather | bytes 104448 | tf_op jit(solution)/shard_map/all_gather | solution.py:19
  467.6 45.8 %while.40 = (s32[]{:T(128)}, f32[96,16]{0,1:T(8,128)}, s32[]{:T(128)}, f32[16]{0:T(128)}, f32[96,16]{0,1:T(8,128)}, /*index=5*/f32[16,96,16]{1,2,0:T(8,128)S(1)}, s32[]{:T(128)}, f32[1]{0:T(128)}, s32[]{:T(128)}) while((s32[]{:T(128)}, f32[96,16]{0,1:T(8,128)}, s32[]{:T(128)}, f32[16]{0:T(128)}, f32[96,16]{0,1:T(8,128)}, ...), condition=%wide.region_4.5_spmd.clone, body=%wide.region_3.4_spmd.clone.sunk | while | flops 7685 | bytes 24729 | solution.py:28
  515.8 13.2 %while.39 = (s32[]{:T(128)}, f32[3,6144,32]{1,2,0:T(8,128)}, f32[3,32,16]{1,0,2:T(4,128)}, f32[3,32,16]{2,1,0:T(8,128)S(1)}, f32[3,32,16]{2,1,0:T(8,128)}, /*index=5*/s32[]{:T(128)}) while((s32[]{:T(128)}, f32[3,6144,32]{1,2,0:T(8,128)}, f32[3,32,16]{1,0,2:T(4,128)}, f32[3,32,16]{2,1,0:T(8,128)S(1)}, f32[3,32,16]{2,1,0:T(8,128)}, ...), condition=%wide.region_6.7_spmd, body=%wide.region_5.6_spmd.sunk | while | flops 37929648 | bytes 3960281 | solution.py:113
  529.0 2.6 add.242
  534.8 6.8 %all-to-all-start.1 = ((bf16[48,128,96]{1,2,0:T(8,128)(2,1)}), bf16[48,128,96]{1,2,0:T(8,128)(2,1)S(1)}, u32[]{:S(2)}, u32[]{:S(2)}) async-start(bf16[48,128,96]{1,2,0:T(8,128)(2,1)} %fusion.39), calls=%async_computation.1 | async-start | bytes 2359296 | tf_op jit(solution)/shard_map/all_to_all | solution.py:163
  542.3 3.6 collective-permute-start
  554.2 31.1 %collective-permute-done = bf16[6,4608]{1,0:T(8,128)(2,1)} collective-permute-done((bf16[6,4608]{1,0:T(8,128)(2,1)}, bf16[6,4608]{1,0:T(8,128)(2,1)}, u32[]{:S(2)}, u32[]{:S(2)}) %collective-permute-start) | collective-permute-done | bytes 55328 | tf_op jit(solution)/shard_map/ppermute | solution.py:14
  585.3 2.4 copy.249
  587.7 11.3 %add_convert_fusion = bf16[128,4608]{0,1:T(8,128)(2,1)S(1)} fusion(bf16[128,4608]{0,1:T(8,128)(2,1)S(1)} %copy.248, bf16[6,4608]{0,1:T(8,128)(2,1)} %copy.249, f32[4608]{0:T(1024)} %broadcast_in_dim.147, f32[4608]{0:T(1024)} %broadcast_in_dim.145, f32[4608]{0:T(1024)} %broadcast_in_dim.143, f32[4608]{0:T(1024)} %broadcast_in_dim.141, ...), kind=kLoop, calls=%fused_computation.125 | loop fusion | flops 23003136 | bytes 2543616 | tf_op jit(solution)/shard_map/convert_element_type | solution.py:136
  (387 shorter events, 165.8 us)
Async XLA Ops:
  0.0 14.8 %copy-start.8 = (bf16[128,4608]{1,0:T(8,128)(2,1)S(1)}, bf16[128,4608]{1,0:T(8,128)(2,1)}, u32[]{:S(2)}) copy-start(bf16[128,4608]{1,0:T(8,128)(2,1)} %param.15) | copy-start | bytes 3538948
  1.6 32.1 %collective-permute-start.2 = (bf16[6,4608]{1,0:T(8,128)(2,1)}, bf16[6,4608]{1,0:T(8,128)(2,1)}, u32[]{:S(2)}, u32[]{:S(2)}) collective-permute-start(bf16[6,4608]{1,0:T(8,128)(2,1)} %slice.460), channel_id=1, source_target_pairs={{0,1},{1,2},{2,3},{3,4},{4,5},{5,6},{6,7},{7,8},{8,9},{9,10},{10,1... | collective-permute-start | bytes 165896 | tf_op jit(solution)/shard_map/ppermute | solution.py:14
  6.6 25.8 %collective-permute-start.1 = (bf16[6,4608]{1,0:T(8,128)(2,1)}, bf16[6,4608]{1,0:T(8,128)(2,1)}, u32[]{:S(2)}, u32[]{:S(2)}) collective-permute-start(bf16[6,4608]{1,0:T(8,128)(2,1)} %slice.439), channel_id=1, source_target_pairs={{0,1},{1,2},{2,3},{3,4},{4,5},{5,6},{6,7},{7,8},{8,9},{9,10},{10,1... | collective-permute-start | bytes 165896 | tf_op jit(solution)/shard_map/ppermute | solution.py:14
  15.6 11.9 %copy-start.16 = (f32[288]{0:T(512)S(1)}, f32[288]{0:T(512)}, u32[]{:S(2)}) copy-start(f32[288]{0:T(512)} %get-tuple-element.334) | copy-start | bytes 3460
  15.6 12.7 %copy-start.15 = (f32[288]{0:T(512)S(1)}, f32[288]{0:T(512)}, u32[]{:S(2)}) copy-start(f32[288]{0:T(512)} %get-tuple-element.335) | copy-start | bytes 3460
  59.9 63.0 %all-to-all-start = ((bf16[128,48,96]{0,2,1:T(8,128)(2,1)}), bf16[128,48,96]{0,2,1:T(8,128)(2,1)S(1)}, u32[]{:S(2)}, u32[]{:S(2)}) async-start(bf16[128,48,96]{0,2,1:T(8,128)(2,1)} %bitcast.11), calls=%async_computation | async-start | bytes 2359296 | tf_op jit(solution)/shard_map/all_to_all | solution.py:148
  122.9 1.7 copy-start.2
  129.4 24.4 %copy-start.6 = (f32[32,16]{0,1:T(8,128)}, f32[32,16]{0,1:T(8,128)S(1)}, u32[]{:S(2)}) copy-start(f32[32,16]{0,1:T(8,128)S(1)} %get-tuple-element.511) | copy-start | bytes 6148 | tf_op jit(solution)/shard_map/while
  129.5 0.6 copy-start.4
  138.5 5.8 copy-start.1
  158.1 1.0 copy-start.10
  221.5 5.1 copy-start
  221.5 5.2 copy-start.5
  221.5 5.2 copy-start.7
  237.3 24.4 %copy-start.6 = (f32[32,16]{0,1:T(8,128)}, f32[32,16]{0,1:T(8,128)S(1)}, u32[]{:S(2)}) copy-start(f32[32,16]{0,1:T(8,128)S(1)} %get-tuple-element.511) | copy-start | bytes 6148 | tf_op jit(solution)/shard_map/while
  237.4 0.6 copy-start.4
  246.4 5.8 copy-start.1
  266.0 1.0 copy-start.10
  329.4 5.1 copy-start
  329.4 5.2 copy-start.5
  329.4 5.2 copy-start.7
  345.2 24.4 %copy-start.6 = (f32[32,16]{0,1:T(8,128)}, f32[32,16]{0,1:T(8,128)S(1)}, u32[]{:S(2)}) copy-start(f32[32,16]{0,1:T(8,128)S(1)} %get-tuple-element.511) | copy-start | bytes 6148 | tf_op jit(solution)/shard_map/while
  345.3 0.6 copy-start.4
  354.3 5.8 copy-start.1
  373.9 1.0 copy-start.10
  437.3 5.1 copy-start
  437.3 5.2 copy-start.5
  437.3 5.2 copy-start.7
  531.6 1.3 copy-start.3
  531.6 1.3 copy-start.17
  534.8 6.8 %copy-start.9 = (bf16[128,4608]{1,0:T(8,128)(2,1)S(1)}, bf16[128,4608]{1,0:T(8,128)(2,1)}, u32[]{:S(2)}) copy-start(bf16[128,4608]{1,0:T(8,128)(2,1)} %param.13) | copy-start | bytes 3538948
  534.8 16.2 %copy-start.14 = (f32[288]{0:T(512)S(1)}, f32[288]{0:T(512)}, u32[]{:S(2)}) copy-start(f32[288]{0:T(512)} %get-tuple-element.342) | copy-start | bytes 3460
  534.8 64.2 %all-to-all-start.1 = ((bf16[48,128,96]{1,2,0:T(8,128)(2,1)}), bf16[48,128,96]{1,2,0:T(8,128)(2,1)S(1)}, u32[]{:S(2)}, u32[]{:S(2)}) async-start(bf16[48,128,96]{1,2,0:T(8,128)(2,1)} %fusion.39), calls=%async_computation.1 | async-start | bytes 2359296 | tf_op jit(solution)/shard_map/all_to_all | solution.py:163
  541.6 10.2 %copy-start.13 = (f32[288]{0:T(512)S(1)}, f32[288]{0:T(512)}, u32[]{:S(2)}) copy-start(f32[288]{0:T(512)} %get-tuple-element.343) | copy-start | bytes 3460
  541.6 11.0 %copy-start.12 = (f32[288]{0:T(512)S(1)}, f32[288]{0:T(512)}, u32[]{:S(2)}) copy-start(f32[288]{0:T(512)} %get-tuple-element.344) | copy-start | bytes 3460
  541.6 11.8 %copy-start.11 = (f32[288]{0:T(512)S(1)}, f32[288]{0:T(512)}, u32[]{:S(2)}) copy-start(f32[288]{0:T(512)} %get-tuple-element.345) | copy-start | bytes 3460
  542.3 43.0 %collective-permute-start = (bf16[6,4608]{1,0:T(8,128)(2,1)}, bf16[6,4608]{1,0:T(8,128)(2,1)}, u32[]{:S(2)}, u32[]{:S(2)}) collective-permute-start(bf16[6,4608]{1,0:T(8,128)(2,1)} %slice.418), channel_id=1, source_target_pairs={{0,1},{1,2},{2,3},{3,4},{4,5},{5,6},{6,7},{7,8},{8,9},{9,10},{10,1... | collective-permute-start | bytes 165896 | tf_op jit(solution)/shard_map/ppermute | solution.py:14
where the time goes:
time: 610 us; the launch traced here: 601 us
  local copies, waits for them, and re-layouts  342 us (56%)
  other arithmetic  78.7 us (13%)
  matrix products  50.8 us (8%)
  waiting for transfers between devices  46.8 us (8%)
  blocking collectives  37.6 us (6%)
  starting transfers between devices  35.1 us (6%)
  loops' own time  9.65 us (2%)
    while x48, local copies, waits for them, and re-layouts  97 us
    pad x39, local copies, waits for them, and re-layouts, modal_local(): _, through = lax.associative_scan(link_blocks, (factor, block_state))  95.9 us
    ppermute x3, waiting for transfers between devices, from_behind(): lax.ppermute(value, axis, [(source, source + steps) for source in range(f...  31.1 us
    broadcast_in_dim x42, local copies, waits for them, and re-layouts, local(): jnp.repeat(featurizer, feature_width // featurizer.shape[2], axis=2)  24.2 us
    convert_element_type x1, other arithmetic, local(): signal_half = (featured[1] * featured[2]).astype(jnp.bfloat16)  23.7 us
    unnamed x1, blocking collectives  22.4 us
    dot_general x3, matrix products, modal_local(): within = jnp.einsum('ijc,bjc->bic', toeplitz, blocks, precision=precise)  20.5 us
    select_n x15, other arithmetic, lap(): jnp.where(position < mine, new, old)  20 us
  transfers between devices with their start and end apart: 5, of which 2 were waited for; matrix products, arithmetic and copies ran while one was open for 9% of the time, Pallas kernels for 0%

commit v1 on v0

v1 whole, which is shorter than its diff:
```python
import functools

import jax
import jax.numpy as jnp
from jax import lax
from jax.experimental import pallas as pl
from jax.experimental.pallas import tpu as pltpu
from jax.sharding import PartitionSpec as P

F32 = jnp.float32
BF16 = jnp.bfloat16
LANES = 128
SUBS = 8
ROWS = 128
STEPS = ROWS // SUBS
MESH = pl.DeviceIdType.MESH


def rounded(value):
    return value.astype(BF16).astype(F32)


def kernel(
    nx, nz, ns, taps_n, modes, tiles,
    q_hbm, k_hbm, v_hbm, taps, rates, coef, skip, out,
    raw, halo, ext, perm, u, y, gate, sx, ends, rx, pre, rowsum, rz, prez, tot, ry, bsend, base, xsend, enter,
    in_sem, hs_sem, hr_sem, xs_sem, xr_sem, zs_sem, zr_sem, ys_sem, yr_sem, bs_sem, br_sem, ws_sem, wr_sem, own_sem,
):
    quarter = tiles // nx
    seq = lax.axis_index("seq")
    cp = lax.axis_index("cp")
    z = cp // nx
    x = cp % nx
    linear = seq * (nx * nz) + cp
    count = nx * nz * ns
    sub = lax.broadcasted_iota(jnp.int32, (SUBS, LANES), 0)

    def device(seq_at, cp_at):
        return {"seq": seq_at, "cp": cp_at}

    after = lax.rem(linear + 1, count)
    before = lax.rem(linear + count - 1, count)
    after_dev = device(after // (nx * nz), after % (nx * nz))
    before_dev = device(before // (nx * nz), before % (nx * nz))

    def at_x(step):
        return device(seq, z * nx + lax.rem(x + step, nx))

    def at_z(step):
        return device(seq, lax.rem(z + step, nz) * nx + x)

    def at_s(step):
        return device(lax.rem(seq + step, ns), cp)

    sources = (q_hbm, k_hbm, v_hbm)
    loads = [pltpu.make_async_copy(sources[m], raw.at[m], in_sem.at[m]) for m in range(3)]
    for m in (1, 2, 0):
        loads[m].start()

    barrier = pltpu.get_barrier_semaphore()
    for target in (after_dev, before_dev):
        pl.semaphore_signal(barrier, inc=1, device_id=target, device_id_type=MESH)
    for step in range(1, nx):
        pl.semaphore_signal(barrier, inc=1, device_id=at_x(step), device_id_type=MESH)

    def greet_z(step, carry):
        pl.semaphore_signal(barrier, inc=1, device_id=at_z(step), device_id_type=MESH)
        return carry

    def greet_s(step, carry):
        pl.semaphore_signal(barrier, inc=1, device_id=at_s(step), device_id_type=MESH)
        return carry

    lax.fori_loop(1, nz, greet_z, 0)
    lax.fori_loop(1, ns, greet_s, 0)
    pl.semaphore_wait(barrier, 2 + (nx - 1) + (nz - 1) + (ns - 1))

    def halo_copy(m):
        return pltpu.make_async_remote_copy(
            src_ref=sources[m].at[pl.ds(ROWS - SUBS, SUBS), :],
            dst_ref=halo.at[m],
            send_sem=hs_sem.at[m],
            recv_sem=hr_sem.at[m],
            device_id=after_dev,
            device_id_type=MESH,
        )

    for m in (1, 2, 0):
        halo_copy(m).start()

    seen = (linear > 0).astype(F32)

    def lanes_of(tile):
        return pl.ds(pl.multiple_of(tile * LANES, LANES), LANES)

    def row(ref, index, lanes):
        return jnp.broadcast_to(ref[index:index + 1, lanes], (SUBS, LANES))

    def featured(m, lanes):
        ext[m, 0:SUBS, :] = halo[m, :, lanes].astype(F32) * seen
        ext[m, SUBS:SUBS + ROWS, :] = raw[m, :, lanes].astype(F32)
        shifted = {
            j: ext[m, pl.ds(SUBS + j, SUBS, stride=STEPS), :] for j in range(1 - taps_n, STEPS)
        }
        weights = [
            jnp.broadcast_to(taps[m, i:i + 1, lanes], (SUBS, LANES)) for i in range(taps_n)
        ]
        result = []
        for j in range(STEPS):
            total = weights[0] * shifted[j]
            for i in range(1, taps_n):
                total = total + weights[i] * shifted[j - i]
            result.append(total)
        return result

    for m in (1, 2):
        loads[m].wait()
        halo_copy(m).wait_recv()

    def first(tile, carry):
        lanes = lanes_of(tile)
        part = tile // quarter
        inner = lanes_of(tile % quarter)
        key = featured(1, lanes)
        value = featured(2, lanes)
        signal = [rounded(key[j] * value[j]) for j in range(STEPS)]
        for j in range(STEPS):
            u[j * SUBS:(j + 1) * SUBS, lanes] = signal[j]
        decay_all = jnp.exp(-rates[:, lanes])
        for r in range(modes):
            a = jnp.broadcast_to(decay_all[r:r + 1], (SUBS, LANES))
            s = signal[0]
            for j in range(1, STEPS):
                s = s * a + signal[j]
            a2 = a * a
            a4 = a2 * a2
            a8 = a4 * a4
            a16 = a8 * a8
            a32 = a16 * a16
            a64 = a32 * a32
            s = s + jnp.where(sub >= 1, a16 * pltpu.roll(s, 1, 0), 0.0)
            s = s + jnp.where(sub >= 2, a32 * pltpu.roll(s, 2, 0), 0.0)
            s = s + jnp.where(sub >= 4, a64 * pltpu.roll(s, 4, 0), 0.0)
            ends[part, r:r + 1, inner] = s[SUBS - 1:SUBS]
            sx[r, :, lanes] = jnp.where(sub >= 1, pltpu.roll(s, 1, 0), 0.0)
        return carry

    lax.fori_loop(0, tiles, first, 0)

    def x_copy(step):
        return pltpu.make_async_remote_copy(
            src_ref=ends.at[lax.rem(x + step, nx)],
            dst_ref=rx.at[step],
            send_sem=xs_sem.at[step],
            recv_sem=xr_sem.at[step],
            device_id=at_x(step),
            device_id_type=MESH,
        )

    for step in range(1, nx):
        x_copy(step).start()
    own = pltpu.make_async_copy(ends.at[x], rx.at[0], own_sem.at[0])
    own.start()

    def second(tile, carry):
        lanes = lanes_of(tile)
        query = featured(0, lanes)
        for j in range(STEPS):
            gate[j * SUBS:(j + 1) * SUBS, lanes] = rounded(query[j])
        decay_all = jnp.exp(-rates[:, lanes])
        power = coef[:, lanes]
        tap = []
        for j in range(STEPS):
            tap.append(jnp.broadcast_to(jnp.sum(power, axis=0, keepdims=True), (SUBS, LANES)))
            power = power * decay_all
        tap[0] = tap[0] + jnp.broadcast_to(skip[:, lanes], (SUBS, LANES))
        signal = [u[j * SUBS:(j + 1) * SUBS, lanes] for j in range(STEPS)]
        for j in range(STEPS):
            total = tap[0] * signal[j]
            for i in range(1, j + 1):
                total = total + tap[i] * signal[j - i]
            y[j * SUBS:(j + 1) * SUBS, lanes] = total
        return carry

    loads[0].wait()
    halo_copy(0).wait_recv()
    lax.fori_loop(0, tiles, second, 0)

    own.wait()
    for step in range(1, nx):
        x_copy(step).wait_recv()

    def slot(position, place, size):
        return lax.rem(place - position + size, size)

    def row_prefix(tile, carry):
        lanes = lanes_of(tile)
        rate = rates[:, lanes_of(x * quarter + tile)]
        factor = jnp.exp(-rate * float(ROWS))
        state = rx[slot(0, x, nx), :, lanes]
        for i in range(1, nx):
            pre[i, :, lanes] = state
            state = factor * state + rx[slot(i, x, nx), :, lanes]
        rowsum[tile] = state
        return carry

    lax.fori_loop(0, quarter, row_prefix, 0)

    owner = z < quarter
    my_tile = lanes_of(x * quarter + lax.rem(z, quarter))

    def z_copy(step):
        return pltpu.make_async_remote_copy(
            src_ref=rowsum.at[lax.rem(lax.rem(z + step, nz), quarter)],
            dst_ref=rz.at[step],
            send_sem=zs_sem.at[step],
            recv_sem=zr_sem.at[step],
            device_id=at_z(step),
            device_id_type=MESH,
        )

    def z_sends(step):
        return lax.rem(z + step, nz) < quarter

    def z_start(step, carry):
        @pl.when(z_sends(step))
        def _():
            z_copy(step).start()
        return carry

    lax.fori_loop(1, nz, z_start, 0)

    def b_copy(step):
        return pltpu.make_async_remote_copy(
            src_ref=bsend.at[lax.rem(z + step, nz)],
            dst_ref=base.at[lax.rem(z, quarter)],
            send_sem=bs_sem.at[step],
            recv_sem=br_sem.at[step],
            device_id=at_z(step),
            device_id_type=MESH,
        )

    def y_copy(step):
        return pltpu.make_async_remote_copy(
            src_ref=tot,
            dst_ref=ry.at[step],
            send_sem=ys_sem.at[step],
            recv_sem=yr_sem.at[step],
            device_id=at_s(step),
            device_id_type=MESH,
        )

    @pl.when(owner)
    def _():
        rate = rates[:, my_tile]
        row_factor = jnp.exp(-rate * float(ROWS * nx))
        group_factor = jnp.exp(-rate * float(ROWS * nx * nz))
        rz[0] = rowsum[lax.rem(z, quarter)]

        def z_wait(step, carry):
            z_copy(step).wait_recv()
            return carry

        lax.fori_loop(1, nz, z_wait, 0)

        def z_join(i, state):
            prez[i] = state
            return row_factor * state + rz[slot(i, z, nz)]

        tot[...] = lax.fori_loop(0, nz, z_join, jnp.zeros((modes, LANES), F32))

        def y_start(step, carry):
            @pl.when(seq + step < ns)
            def _():
                y_copy(step).start()
            return carry

        lax.fori_loop(1, ns, y_start, 0)

        def y_wait(step, carry):
            y_copy(step).wait_recv()
            return carry

        lax.fori_loop(1, seq + 1, y_wait, 0)

        def y_join(i, state):
            return group_factor * state + ry[seq - i]

        group = lax.fori_loop(0, seq, y_join, jnp.zeros((modes, LANES), F32))

        def b_make(i, grown):
            bsend[i] = prez[i] + grown
            return grown * row_factor

        lax.fori_loop(0, nz, b_make, group)
        base[lax.rem(z, quarter)] = bsend[z]

        def b_start(step, carry):
            b_copy(step).start()
            return carry

        lax.fori_loop(1, nz, b_start, 0)

    def b_comes(step):
        return lax.rem(z - step + nz, nz) < quarter

    def b_wait(step, carry):
        @pl.when(b_comes(step))
        def _():
            b_copy(step).wait_recv()
        return carry

    lax.fori_loop(1, nz, b_wait, 0)

    def spread(tile, carry):
        lanes = lanes_of(tile)
        rate = rates[:, lanes_of(x * quarter + tile)]
        factor = jnp.exp(-rate * float(ROWS))
        grown = base[tile]
        xsend[0, :, lanes] = grown
        for i in range(1, nx):
            grown = grown * factor
            xsend[i, :, lanes] = pre[i, :, lanes] + grown
        return carry

    lax.fori_loop(0, quarter, spread, 0)

    def w_copy(step):
        return pltpu.make_async_remote_copy(
            src_ref=xsend.at[lax.rem(x + step, nx)],
            dst_ref=enter.at[x],
            send_sem=ws_sem.at[step],
            recv_sem=wr_sem.at[step],
            device_id=at_x(step),
            device_id_type=MESH,
        )

    for step in range(1, nx):
        w_copy(step).start()
    own_back = pltpu.make_async_copy(xsend.at[x], enter.at[x], own_sem.at[1])
    own_back.start()
    own_back.wait()
    for step in range(1, nx):
        w_copy(step).wait_recv()

    def third(tile, carry):
        lanes = lanes_of(tile)
        part = tile // quarter
        inner = lanes_of(tile % quarter)
        decay_all = jnp.exp(-rates[:, lanes])
        lead_all = coef[:, lanes] * decay_all
        enter_all = enter[part, :, inner]
        acc = [y[j * SUBS:(j + 1) * SUBS, lanes] for j in range(STEPS)]
        for r in range(modes):
            a = jnp.broadcast_to(decay_all[r:r + 1], (SUBS, LANES))
            a2 = a * a
            a4 = a2 * a2
            a8 = a4 * a4
            a16 = a8 * a8
            a32 = a16 * a16
            a64 = a32 * a32
            grow = (
                jnp.where(sub % 2 == 1, a16, 1.0)
                * jnp.where((sub // 2) % 2 == 1, a32, 1.0)
                * jnp.where(sub >= 4, a64, 1.0)
            )
            g = sx[r, :, lanes] + grow * jnp.broadcast_to(enter_all[r:r + 1], (SUBS, LANES))
            g = g * jnp.broadcast_to(lead_all[r:r + 1], (SUBS, LANES))
            for j in range(STEPS):
                acc[j] = acc[j] + g
                if j + 1 < STEPS:
                    g = g * a
        for j in range(STEPS):
            product = gate[j * SUBS:(j + 1) * SUBS, lanes] * rounded(acc[j])
            perm[pl.ds(j, SUBS, stride=STEPS), :] = product
        out[:, lanes] = perm[...].astype(BF16)
        return carry

    lax.fori_loop(0, tiles, third, 0)

    for m in range(3):
        halo_copy(m).wait_send()
    for step in range(1, nx):
        x_copy(step).wait_send()
        w_copy(step).wait_send()

    def z_drain(step, carry):
        @pl.when(z_sends(step))
        def _():
            z_copy(step).wait_send()
        return carry

    lax.fori_loop(1, nz, z_drain, 0)

    @pl.when(owner)
    def _():
        def b_drain(step, carry):
            b_copy(step).wait_send()
            return carry

        lax.fori_loop(1, nz, b_drain, 0)

        def y_drain(step, carry):
            @pl.when(seq + step < ns)
            def _():
                y_copy(step).wait_send()
            return carry

        lax.fori_loop(1, ns, y_drain, 0)


def local(nx, nz, ns, query, key_proj, value_proj, featurizer, rates, residues, skip):
    row_count, width = query.shape
    taps_n = featurizer.shape[1]
    modes = rates.shape[0]
    tiles = width // LANES
    quarter = tiles // nx
    taps = jnp.repeat(featurizer, width // featurizer.shape[2], axis=2)
    coef = residues * jnp.sqrt(-jnp.expm1(-2.0 * rates) / modes)
    vm = pltpu.VMEM
    dma = pltpu.SemaphoreType.DMA
    any_spec = pl.BlockSpec(memory_space=pl.ANY)
    vmem_spec = pl.BlockSpec(memory_space=pltpu.VMEM)
    part = quarter * LANES
    return pl.pallas_call(
        functools.partial(kernel, nx, nz, ns, taps_n, modes, tiles),
        out_shape=jax.ShapeDtypeStruct((row_count, width), BF16),
        in_specs=[any_spec] * 3 + [vmem_spec] * 4,
        out_specs=vmem_spec,
        scratch_shapes=[
            vm((3, row_count, width), BF16),
            vm((3, SUBS, width), BF16),
            vm((3, SUBS + row_count, LANES), F32),
            vm((row_count, LANES), F32),
            vm((row_count, width), F32),
            vm((row_count, width), F32),
            vm((row_count, width), F32),
            vm((modes, SUBS, width), F32),
            vm((nx, modes, part), F32),
            vm((nx, modes, part), F32),
            vm((nx, modes, part), F32),
            vm((quarter, modes, LANES), F32),
            vm((nz, modes, LANES), F32),
            vm((nz, modes, LANES), F32),
            vm((modes, LANES), F32),
            vm((ns, modes, LANES), F32),
            vm((nz, modes, LANES), F32),
            vm((quarter, modes, LANES), F32),
            vm((nx, modes, part), F32),
            vm((nx, modes, part), F32),
            dma((3,)),
            dma((3,)),
            dma((3,)),
            dma((nx,)),
            dma((nx,)),
            dma((nz,)),
            dma((nz,)),
            dma((ns,)),
            dma((ns,)),
            dma((nz,)),
            dma((nz,)),
            dma((nx,)),
            dma((nx,)),
            dma((2,)),
        ],
        compiler_params=pltpu.CompilerParams(
            collective_id=0, has_side_effects=True, vmem_limit_bytes=48 << 20
        ),
    )(query, key_proj, value_proj, taps, rates, coef, skip.reshape(1, width))


def solution(mesh):
    nx = 4
    ns = mesh.shape["seq"]
    nz = mesh.shape["cp"] // nx
    rows = P(("seq", "cp"), None)
    return jax.shard_map(
        functools.partial(local, nx, nz, ns),
        mesh=mesh,
        in_specs=(rows, rows, rows, P(), P(), P(), P()),
        out_specs=rows,
        check_vma=False,
    )
```

time: 610 us -> 81 us (0.13); the launches traced: 601 us -> 80.8 us
  local copies, waits for them, and re-layouts: 342 us -> 8.77 us
  other arithmetic: 78.7 us -> 0.18 us
  Pallas kernels: 0 us -> 71.7 us
  matrix products: 50.8 us -> 0 us
  waiting for transfers between devices: 46.8 us -> 0 us
  blocking collectives: 37.6 us -> 0 us
  starting transfers between devices: 35.1 us -> 0 us
  loops' own time: 9.65 us -> 0 us
    while x49 -> x0, local copies, waits for them, and re-layouts: 97.8 us -> none
    pad x39 -> x0, local copies, waits for them, and re-layouts: 95.9 us -> none  [modal_local(): _, through = lax.associative_scan(link_blocks, (factor, block_state))]
    pallas_call x0 -> x1, Pallas kernels: none -> 71.7 us  [local(): pl.pallas_call(functools.partial(kernel, nx, nz, ns, taps_n, modes, tiles...]
    dot_general x12 -> x0, matrix products: 50.8 us -> none  [the longest x3 20.5 us: modal_local(): within = jnp.einsum('ijc,bjc->bic', toeplitz, blocks, precision=precise)]
    convert_element_type x4 -> x0, other arithmetic: 37.3 us -> none  [the longest x1 23.7 us: local(): signal_half = (featured[1] * featured[2]).astype(jnp.bfloat16)]
    ppermute x3 -> x0, waiting for transfers between devices: 31.1 us -> none  [from_behind(): lax.ppermute(value, axis, [(source, source + steps) for source in range(f...]
    dynamic_slice x29 -> x0, local copies, waits for them, and re-layouts: 30.6 us -> none  [the longest x15 17.5 us: lap(): longer = join(so_far, jax.tree.map(lambda part: part[position], pieces))]
    broadcast_in_dim x48 -> x1, local copies, waits for them, and re-layouts: 31.5 us -> 2.88 us  [local(): taps = jnp.repeat(featurizer, width // featurizer.shape[2], axis=2)]
  transfers between devices with their start and end apart: 5 -> 0, of which waited for: 2 -> 0; matrix products, arithmetic and copies ran while one was open for 9% -> 0% of each run, Pallas kernels for 0% -> 0%
where the time goes in v1:
time: 81 us; the launch traced here: 80.8 us
  Pallas kernels  71.7 us (89%)
  local copies, waits for them, and re-layouts  8.77 us (11%)
    pallas_call x1, Pallas kernels, local(): pl.pallas_call(functools.partial(kernel, nx, nz, ns, taps_n, modes, tiles...  71.7 us
    reshape x1, local copies, waits for them, and re-layouts, local(): taps = jnp.repeat(featurizer, width // featurizer.shape[2], axis=2)  3.57 us
    broadcast_in_dim x1, local copies, waits for them, and re-layouts, local(): taps = jnp.repeat(featurizer, width // featurizer.shape[2], axis=2)  2.88 us
    unnamed x13, local copies, waits for them, and re-layouts  2.3 us

profile of v1, /device:TPU:56, one launch (start us, length us, event | category | flops | bytes accessed | tf_op | source)
XLA Modules:
  0.0 80.8 jit_solution(1239148113964681186)
XLA Ops:
  0.0 2.9 %broadcast_in_dim.3 = f32[3,7,288,16]{3,2,1,0:T(8,128)} broadcast(f32[3,7,288]{2,1,0:T(8,128)} %param.10), dimensions={0,1,2} | broadcast | bytes 411264 | tf_op jit(solution)/shard_map/broadcast_in_dim | solution.py:418
  2.9 0.0 copy-start.3
  2.9 0.0 copy-start.4
  2.9 0.0 copy-start.5
  2.9 0.0 copy-start
  2.9 0.0 copy-start.1
  2.9 3.6 %reshape.6.taps = f32[3,7,4608]{2,1,0:T(8,128)S(1)} reshape(f32[3,7,288,16]{3,2,1,0:T(8,128)} %broadcast_in_dim.3) | data formatting | bytes 774144 | tf_op jit(solution)/shard_map/reshape | solution.py:418
  6.5 0.0 copy-done.3
  6.5 0.0 copy-done.4
  6.5 0.2 sqrt_multiply_fusion.coef
  6.7 0.0 copy-done.5
  6.7 0.0 copy-done
  6.7 0.0 copy-done.1
  6.8 0.0 copy-start.2
  6.8 1.3 %copy-done.2 = bf16[128,4608]{1,0:T(8,128)(2,1)S(1)} copy-done((bf16[128,4608]{1,0:T(8,128)(2,1)S(1)}, bf16[128,4608]{1,0:T(8,128)(2,1)}, u32[]{:S(2)}) %copy-start.2) | copy-done | bytes 1179672
  8.0 71.7 %shard_map.73 = bf16[128,4608]{1,0:T(8,128)(2,1)S(1)} custom-call(bf16[128,4608]{1,0:T(8,128)(2,1)S(1)} %copy-done, bf16[128,4608]{1,0:T(8,128)(2,1)S(1)} %copy-done.1, bf16[128,4608]{1,0:T(8,128)(2,1)S(1)} %copy-done.2, f32[3,7,4608]{2,1,0:T(8,128)S(1)} %reshape.6.taps, f32[16,4608]{1,0:T(8,128)S(1)} %copy-done.3, f32[16,4608]{1,0:T(8,128)S(1)} %sqrt_multiply_fusion.coef, ...), custom_call_target="tpu_custom_call" | custom-call | tf_op jit(solution)/shard_map/pallas_call | solution.py:425
  79.7 1.0 %copy.9 = bf16[128,4608]{1,0:T(8,128)(2,1)} copy(bf16[128,4608]{1,0:T(8,128)(2,1)S(1)} %shard_map.73) | data formatting | bytes 2359296
  (1 shorter events, 0.0 us)
Async XLA Ops:
  2.9 3.6 %copy-start.3 = (f32[16,4608]{1,0:T(8,128)S(1)}, f32[16,4608]{1,0:T(8,128)}, u32[]{:S(2)}) copy-start(f32[16,4608]{1,0:T(8,128)} %rates.1) | copy-start | bytes 884740
  2.9 3.6 %copy-start.4 = (f32[16,4608]{1,0:T(8,128)S(1)}, f32[16,4608]{1,0:T(8,128)}, u32[]{:S(2)}) copy-start(f32[16,4608]{1,0:T(8,128)} %param.12) | copy-start | bytes 884740
  2.9 3.8 %copy-start.5 = (f32[4608]{0:T(1024)S(1)}, f32[4608]{0:T(1024)}, u32[]{:S(2)}) copy-start(f32[4608]{0:T(1024)} %param.13) | copy-start | bytes 55300
  2.9 3.8 %copy-start = (bf16[128,4608]{1,0:T(8,128)(2,1)S(1)}, bf16[128,4608]{1,0:T(8,128)(2,1)}, u32[]{:S(2)}) copy-start(bf16[128,4608]{1,0:T(8,128)(2,1)} %q_hbm.1) | copy-start | bytes 3538948
  2.9 3.8 %copy-start.1 = (bf16[128,4608]{1,0:T(8,128)(2,1)S(1)}, bf16[128,4608]{1,0:T(8,128)(2,1)}, u32[]{:S(2)}) copy-start(bf16[128,4608]{1,0:T(8,128)(2,1)} %k_hbm.1) | copy-start | bytes 3538948
  6.8 1.3 %copy-start.2 = (bf16[128,4608]{1,0:T(8,128)(2,1)S(1)}, bf16[128,4608]{1,0:T(8,128)(2,1)}, u32[]{:S(2)}) copy-start(bf16[128,4608]{1,0:T(8,128)(2,1)} %v_hbm.1) | copy-start | bytes 3538948
